TPU v7x, 32 devices: a whole 2x2x4 slice. The times are simulated.
32 devices in a mesh: dom: 8 (over z, y), rhs: 4 (over x, core).
Axes of the slice: x: 2, y: 2, z: 4, core: 2. Of those that a mesh axis runs over, the one named last changes fastest.
Arguments:
- tile_values: float32 [2048, 128, 128], P(('dom', 'rhs')), may hold values from -1 to 3, as said below
- tile_rows: int32 [2048], P(('dom', 'rhs')), may hold values from -1 to 31, as said below
- tile_cols: int32 [2048], P(('dom', 'rhs')), may hold values from 0 to 39, as said below
- send_lists: int32 [8, 2, 4], P('dom'), may hold values from 0 to 31, as said below
- replace_flags: int32 [4], replicated, may hold values from 0 to 1, as said below
- right_side: float32 [4, 256, 128], P(None, ('dom', 'rhs')), may hold values from -25 to 25
- start_iterate: float32 [4, 256, 128], P(None, ('dom', 'rhs')), may hold values from -25 to 25
- start_residual: float32 [4, 256, 128], P(None, ('dom', 'rhs')), may hold values from -25 to 25
- start_direction: float32 [4, 256, 128], P(None, ('dom', 'rhs')), may hold values from -25 to 25
Outputs:
- new_iterate: float32 [4, 256, 128], P(None, ('dom', 'rhs'))
- new_residual: float32 [4, 256, 128], P(None, ('dom', 'rhs'))
- new_direction: float32 [4, 256, 128], P(None, ('dom', 'rhs'))
Inputs may be any that keep to these rules, and one draw needn't show every extreme that they name: `tile_values`: the matrix assembled from all used tile slots is symmetric positive definite. `tile_rows`: -1 marks an empty slot; a used slot of the device with indices (d, r) names a block row from r * 8 to (r + 1) * 8 - 1 of partition d. `tile_cols`: 0 in empty slots. `send_lists`: the 8 entries of one partition are distinct. `replace_flags`: at least one load case is flagged and at least one is not.
All inputs are finite; a program needn't handle non-finite values.
Results may differ from a plain program's by a relative error of at most 0.0003.
Values sent between devices are 32-bit elements; how exact they have to be, the bound alone decides.
A program may use at most 64 MiB of HBM per device.

v0:
```python
import jax
import jax.numpy as jnp
import numpy as np
from jax import lax
from jax.sharding import PartitionSpec as P

SSTEP = 3
highest = lax.Precision.HIGHEST


def with_halo(x, sides, width):
    for axis, dim in sides:
        size, length = (lax.axis_size(axis), x.shape[dim])
        up = [(i, (i + 1) % size) for i in range(size - 1)]
        down = [(j, i) for i, j in up]
        last = lax.slice_in_dim(x, length - width, length, axis=dim)
        first = lax.slice_in_dim(x, 0, width, axis=dim)
        before = lax.ppermute(last, axis, up)
        after = lax.ppermute(first, axis, down)
        x = jnp.concatenate([before, x, after], axis=dim)
    return x


def shift_table(basis_steps):
    basis_width = 2 * basis_steps + 1
    shift_matrix = np.zeros((basis_width, basis_width), np.float32)
    for position in range(basis_steps):
        shift_matrix[position + 1, position] = 1.0
    for position in range(basis_steps - 1):
        shift_matrix[basis_steps + 2 + position, basis_steps + 1 + position] = 1.0
    return shift_matrix


def coefficients(gram_matrix, basis_steps):
    shift_matrix = jnp.asarray(shift_table(basis_steps))
    case_count = gram_matrix.shape[0]
    basis_width = gram_matrix.shape[1]
    eye_matrix = jnp.eye(basis_width, dtype=jnp.float32)
    direction = jnp.broadcast_to(eye_matrix[0], (case_count, basis_width))
    residual = jnp.broadcast_to(eye_matrix[basis_steps + 1], (case_count, basis_width))
    iterate = jnp.zeros((case_count, basis_width), jnp.float32)

    def quadratic(first_vec, second_vec):
        return jnp.einsum("ci,cij,cj->c", first_vec, gram_matrix, second_vec, precision=highest)

    res_norm = quadratic(residual, residual)
    for inner_step in range(basis_steps):
        mapped = jnp.einsum("ij,cj->ci", shift_matrix, direction, precision=highest)
        step_size = res_norm / quadratic(direction, mapped)
        iterate = iterate + step_size[:, None] * direction
        residual = residual - step_size[:, None] * mapped
        next_norm = quadratic(residual, residual)
        direction = residual + (next_norm / res_norm)[:, None] * direction
        res_norm = next_norm
    return (iterate, residual, direction)


def combine(basis_stack, weights):
    return jnp.einsum("icbt,ci->cbt", basis_stack, weights, precision=highest)


def multiply(extended, tile_values, tile_rows, tile_cols, row_start, row_count):
    picked = jnp.take(extended, tile_cols, axis=2)
    product = jnp.einsum("tij,kctj->kcti", tile_values, picked, precision=highest)
    wanted = row_start + lax.iota(jnp.int32, row_count)
    onehot = (tile_rows[:, None] == wanted[None, :]).astype(jnp.float32)
    return jnp.einsum("tb,kcti->kcbi", onehot, product, precision=highest)


def extend(whole_part, own_sends, ghost_width):
    outgoing = jnp.take(whole_part, own_sends, axis=2)
    ghost_rims = with_halo(outgoing, (("dom", 2),), ghost_width)
    return jnp.concatenate(
        [whole_part, ghost_rims[:, :, :ghost_width], ghost_rims[:, :, -ghost_width:]], axis=2
    )


def basis_from(apply_operator, direction, residual, carried):
    direction_powers = [direction]
    residual_powers = [residual]
    carried_image = None
    for power_step in range(SSTEP):
        members = [direction_powers[-1]]
        if power_step < SSTEP - 1:
            members.append(residual_powers[-1])
        if power_step == 0:
            members = members + carried
        mapped = apply_operator(jnp.stack(members))
        direction_powers.append(mapped[0])
        if power_step < SSTEP - 1:
            residual_powers.append(mapped[1])
        if power_step == 0 and carried:
            carried_image = mapped[-1]
    return (jnp.stack(direction_powers + residual_powers), carried_image)


def body(
    tile_values,
    tile_rows,
    tile_cols,
    send_lists,
    replace_flags,
    right_side,
    start_iterate,
    start_residual,
    start_direction,
):
    ghost_width = send_lists.shape[2]
    own_sends = send_lists[0].reshape(2 * ghost_width)
    own_rows = start_residual.shape[1]
    right_part, iterate_part, residual_part, direction_part = (
        right_side,
        start_iterate,
        start_residual,
        start_direction,
    )
    row_start = lax.axis_index("rhs") * own_rows

    def apply_operator(stacked):
        whole_part = lax.all_gather(stacked, "rhs", axis=2, tiled=True)
        return multiply(
            extend(whole_part, own_sends, ghost_width),
            tile_values,
            tile_rows,
            tile_cols,
            row_start,
            own_rows,
        )

    basis_stack, start_image = basis_from(
        apply_operator, direction_part, residual_part, [iterate_part]
    )
    gram_matrix = lax.psum(
        jnp.einsum("icbt,jcbt->cij", basis_stack, basis_stack, precision=highest), ("dom", "rhs")
    )
    iterate_coef, residual_coef, direction_coef = coefficients(gram_matrix, SSTEP)
    new_iterate = iterate_part + combine(basis_stack, iterate_coef)
    recursive = combine(basis_stack, residual_coef)
    new_direction = combine(basis_stack, direction_coef)
    shifted = jnp.einsum(
        "ij,cj->ci", jnp.asarray(shift_table(SSTEP)), iterate_coef, precision=highest
    )
    iterate_image = start_image + combine(basis_stack, shifted)
    replaced = right_part - iterate_image
    new_residual = jnp.where(replace_flags[:, None, None] > 0, replaced, recursive)
    return (new_iterate, new_residual, new_direction)


def solution(mesh):
    placed = (
        P(("dom", "rhs"), None, None),
        P(("dom", "rhs")),
        P(("dom", "rhs")),
        P("dom", None, None),
        P(),
        P(None, ("dom", "rhs"), None),
        P(None, ("dom", "rhs"), None),
        P(None, ("dom", "rhs"), None),
        P(None, ("dom", "rhs"), None),
    )
    return jax.shard_map(
        body,
        mesh=mesh,
        in_specs=placed,
        out_specs=(
            P(None, ("dom", "rhs"), None),
            P(None, ("dom", "rhs"), None),
            P(None, ("dom", "rhs"), None),
        ),
        check_vma=False,
    )
```

profile of v0, /device:TPU:0, one launch (start us, length us, event | category | flops | bytes accessed | tf_op | source)
XLA Modules:
  0.0 127.8 jit_solution(9150678838584309851)
XLA Ops:
  0.6 0.8 reshape_squeeze.6
  1.4 0.8 reshape_squeeze.5
  2.2 0.8 pad_maximum_fusion.2
  2.9 6.8 %all_gather.9 = f32[3,4,32,128]{3,2,1,0:T(8,128)S(1)} all-gather(f32[3,4,8,128]{3,2,1,0:T(8,128)S(1)} %pad_maximum_fusion.2), channel_id=1, replica_groups=mesh['dom'=8,'rhs'=4] {'rhs'}, dimensions={2}, use_global_device_ids=true | all-gather | bytes 245760 | tf_op jit(solution)/shard_map/all_gather | solution.py:120
  9.8 0.1 copy.18
  9.9 0.6 gather_fusion
  10.5 0.1 fusion.31
  10.6 3.6 %collective-permute-start = (f32[3,4,4,128]{3,2,1,0:T(4,128)S(1)}, f32[3,4,4,128]{3,2,1,0:T(4,128)S(1)}, u32[]{:S(2)}, u32[]{:S(2)}) collective-permute-start(f32[3,4,4,128]{3,2,1,0:T(4,128)S(1)} %get-tuple-element.3), channel_id=1, source_target_pairs={{0,4},{4,8},{8,12},{12,16},{16,20},{20,24},{24,28},{1,5},{5,9},{9,... | collective-permute-start | bytes 73736 | tf_op jit(solution)/shard_map/ppermute | solution.py:18
  14.3 1.3 %collective-permute-start.1 = (f32[3,4,4,128]{3,2,1,0:T(4,128)S(1)}, f32[3,4,4,128]{3,2,1,0:T(4,128)S(1)}, u32[]{:S(2)}, u32[]{:S(2)}) collective-permute-start(f32[3,4,4,128]{3,2,1,0:T(4,128)S(1)} %get-tuple-element.4), channel_id=1, source_target_pairs={{4,0},{8,4},{12,8},{16,12},{20,16},{24,20},{28,24},{5,1},{9,5},{13... | collective-permute-start | bytes 73736 | tf_op jit(solution)/shard_map/ppermute | solution.py:19
  15.6 0.7 compare_select_fusion.2
  16.2 0.7 compare_and_fusion.1
  16.9 0.7 constant_dynamic-update-slice_fusion.2
  17.6 2.3 %collective-permute-done.1 = f32[3,4,4,128]{3,2,1,0:T(4,128)S(1)} collective-permute-done((f32[3,4,4,128]{3,2,1,0:T(4,128)S(1)}, f32[3,4,4,128]{3,2,1,0:T(4,128)S(1)}, u32[]{:S(2)}, u32[]{:S(2)}) %collective-permute-start.1) | collective-permute-done | bytes 24608 | tf_op jit(solution)/shard_map/ppermute | solution.py:19
  20.1 0.8 gather_fusion.1
  20.9 8.7 %fusion.2 = f32[64,3,4,128]{3,2,1,0:T(4,128)S(1)} fusion(f32[64,128,128]{2,1,0:T(8,128)} %param.11, f32[64,3,4,128]{3,2,1,0:T(4,128)S(1)} %gather_fusion.1, pred[64]{0:T(512)(128)(4,1)S(1)} %compare_and_fusion.1), kind=kOutput, calls=%fused_computation.8 | convolution fusion | flops 151093248 | bytes 4980800 | tf_op jit(solution)/shard_map/tij,kctj->kcti/dot_general | solution.py:64
  29.6 0.3 convolution_bitcast_fusion.1
  29.9 5.4 %all_gather.10 = f32[2,4,32,128]{3,2,1,0:T(8,128)S(1)} all-gather(f32[2,4,8,128]{3,2,1,0:T(8,128)S(1)} %stack.26), channel_id=1, replica_groups=mesh['dom'=8,'rhs'=4] {'rhs'}, dimensions={2}, use_global_device_ids=true | all-gather | bytes 163840 | tf_op jit(solution)/shard_map/all_gather | solution.py:120
  35.3 0.1 copy.21
  35.4 0.6 gather_fusion.2
  36.0 0.1 fusion.32
  36.1 4.3 %collective-permute-start.2 = (f32[2,4,4,128]{3,2,1,0:T(4,128)S(1)}, f32[2,4,4,128]{3,2,1,0:T(4,128)S(1)}, u32[]{:S(2)}, u32[]{:S(2)}) collective-permute-start(f32[2,4,4,128]{3,2,1,0:T(4,128)S(1)} %get-tuple-element.7), channel_id=1, source_target_pairs={{0,4},{4,8},{8,12},{12,16},{16,20},{20,24},{24,28},{1,5},{5,9},{9,... | collective-permute-start | bytes 49160 | tf_op jit(solution)/shard_map/ppermute | solution.py:18
  40.4 1.3 %collective-permute-start.3 = (f32[2,4,4,128]{3,2,1,0:T(4,128)S(1)}, f32[2,4,4,128]{3,2,1,0:T(4,128)S(1)}, u32[]{:S(2)}, u32[]{:S(2)}) collective-permute-start(f32[2,4,4,128]{3,2,1,0:T(4,128)S(1)} %get-tuple-element.8), channel_id=1, source_target_pairs={{4,0},{8,4},{12,8},{16,12},{20,16},{24,20},{28,24},{5,1},{9,5},{13... | collective-permute-start | bytes 49160 | tf_op jit(solution)/shard_map/ppermute | solution.py:19
  41.7 0.1 collective-permute-done.2
  41.8 4.2 %collective-permute-done.3 = f32[2,4,4,128]{3,2,1,0:T(4,128)S(1)} collective-permute-done((f32[2,4,4,128]{3,2,1,0:T(4,128)S(1)}, f32[2,4,4,128]{3,2,1,0:T(4,128)S(1)}, u32[]{:S(2)}, u32[]{:S(2)}) %collective-permute-start.3) | collective-permute-done | bytes 16416 | tf_op jit(solution)/shard_map/ppermute | solution.py:19
  46.1 0.7 gather_fusion.3
  46.9 8.4 %fusion = f32[64,2,4,128]{3,2,1,0:T(4,128)S(1)} fusion(f32[64,128,128]{2,1,0:T(8,128)} %param.11, f32[64,2,4,128]{3,2,1,0:T(4,128)S(1)} %gather_fusion.3, pred[64]{0:T(512)(128)(4,1)S(1)} %compare_and_fusion.1), kind=kOutput, calls=%fused_computation.6 | convolution fusion | flops 100728832 | bytes 4718656 | tf_op jit(solution)/shard_map/tij,kctj->kcti/dot_general | solution.py:64
  55.3 0.2 convolution_bitcast_fusion.2
  55.5 5.2 %all_gather.11 = f32[1,4,32,128]{3,2,1,0:T(8,128)S(1)} all-gather(f32[1,4,8,128]{3,2,1,0:T(8,128)S(1)} %get-tuple-element.5), channel_id=1, replica_groups=mesh['dom'=8,'rhs'=4] {'rhs'}, dimensions={2}, use_global_device_ids=true | all-gather | bytes 81920 | tf_op jit(solution)/shard_map/all_gather | solution.py:120
  60.8 0.6 gather_fusion.4
  61.4 0.1 bitcast_select_fusion
  61.5 3.4 %collective-permute-start.4 = (f32[1,4,4,128]{3,2,1,0:T(4,128)S(1)}, f32[1,4,4,128]{3,2,1,0:T(4,128)S(1)}, u32[]{:S(2)}, u32[]{:S(2)}) collective-permute-start(f32[1,4,4,128]{3,2,1,0:T(4,128)S(1)} %get-tuple-element.9), channel_id=1, source_target_pairs={{0,4},{4,8},{8,12},{12,16},{16,20},{20,24},{24,28},{1,5},{5,9},{9,... | collective-permute-start | bytes 24584 | tf_op jit(solution)/shard_map/ppermute | solution.py:18
  64.9 1.3 %collective-permute-start.5 = (f32[1,4,4,128]{3,2,1,0:T(4,128)S(1)}, f32[1,4,4,128]{3,2,1,0:T(4,128)S(1)}, u32[]{:S(2)}, u32[]{:S(2)}) collective-permute-start(f32[1,4,4,128]{3,2,1,0:T(4,128)S(1)} %get-tuple-element.10), channel_id=1, source_target_pairs={{4,0},{8,4},{12,8},{16,12},{20,16},{24,20},{28,24},{5,1},{9,5},{13... | collective-permute-start | bytes 24584 | tf_op jit(solution)/shard_map/ppermute | solution.py:19
  66.3 4.2 %collective-permute-done.5 = f32[1,4,4,128]{3,2,1,0:T(4,128)S(1)} collective-permute-done((f32[1,4,4,128]{3,2,1,0:T(4,128)S(1)}, f32[1,4,4,128]{3,2,1,0:T(4,128)S(1)}, u32[]{:S(2)}, u32[]{:S(2)}) %collective-permute-start.5) | collective-permute-done | bytes 8224 | tf_op jit(solution)/shard_map/ppermute | solution.py:19
  70.5 0.7 gather_fusion.5
  71.2 8.4 %convolution_bitcast_fusion = f32[4,64,128]{2,0,1:T(4,128)S(1)} fusion(f32[64,128,128]{2,1,0:T(8,128)} %param.11, f32[64,4,128]{2,1,0:T(4,128)S(1)} %gather_fusion.5, pred[64]{0:T(512)(128)(4,1)S(1)} %compare_and_fusion.1), kind=kOutput, calls=%fused_computation.10 | convolution fusion | flops 50364416 | bytes 4456512 | tf_op jit(solution)/shard_map/tij,kctj->kcti/dot_general | solution.py:64
  79.5 0.2 fusion.4
  79.8 0.4 convolution_bitcast_fusion.3
  80.2 41.2 %psum.7 = f32[4,7,7]{2,1,0:T(8,128)S(1)} all-reduce(f32[4,7,7]{2,1,0:T(8,128)S(1)} %convolution_bitcast_fusion.3), channel_id=1, replica_groups=mesh['dom'=8,'rhs'=4] {'dom','rhs'}, use_global_device_ids=true, to_apply=%region_0.1 | all-reduce | flops 196 | bytes 1568 | tf_op jit(solution)/shard_map/psum | solution.py:133
  121.4 0.2 fusion.53
  121.6 0.1 multiply_reduce_fusion.6
  121.7 0.2 fusion.54
  121.9 0.2 multiply_reduce_fusion.5
  122.2 0.1 multiply_subtract_fusion.2
  122.2 0.2 fusion.55
  122.4 0.2 multiply_reduce_fusion.4
  122.6 0.1 multiply_add_fusion.3
  122.7 0.2 fusion.56
  122.8 0.2 multiply_reduce_fusion.3
  123.1 0.1 multiply_subtract_fusion.1
  123.2 0.2 fusion.57
  123.3 0.1 multiply_reduce_fusion.2
  123.5 0.1 multiply_add_fusion.2
  123.6 0.2 fusion.58
  123.7 0.2 multiply_reduce_fusion.1
  124.1 0.2 fusion.60
  124.2 0.1 multiply_reduce_fusion
  124.4 0.1 multiply_add_fusion
  124.4 0.9 fusion.15
  125.4 0.1 fusion.59
  125.5 0.3 fusion.19
  125.8 0.3 fusion.17
  126.2 0.3 fusion.21
  126.5 0.6 add.82
  127.1 0.7 fusion.35
  (47 shorter events, 0.5 us)
Async XLA Ops:
  0.6 29.0 %copy-start.4 = (s32[64]{0:T(128)S(1)}, s32[64]{0:T(128)}, u32[]{:S(2)}) copy-start(s32[64]{0:T(128)} %param.12) | copy-start | bytes 772
  10.6 7.0 %collective-permute-start = (f32[3,4,4,128]{3,2,1,0:T(4,128)S(1)}, f32[3,4,4,128]{3,2,1,0:T(4,128)S(1)}, u32[]{:S(2)}, u32[]{:S(2)}) collective-permute-start(f32[3,4,4,128]{3,2,1,0:T(4,128)S(1)} %get-tuple-element.3), channel_id=1, source_target_pairs={{0,4},{4,8},{8,12},{12,16},{16,20},{20,24},{24,28},{1,5},{5,9},{9,... | collective-permute-start | bytes 73736 | tf_op jit(solution)/shard_map/ppermute | solution.py:18
  14.3 5.7 %collective-permute-start.1 = (f32[3,4,4,128]{3,2,1,0:T(4,128)S(1)}, f32[3,4,4,128]{3,2,1,0:T(4,128)S(1)}, u32[]{:S(2)}, u32[]{:S(2)}) collective-permute-start(f32[3,4,4,128]{3,2,1,0:T(4,128)S(1)} %get-tuple-element.4), channel_id=1, source_target_pairs={{4,0},{8,4},{12,8},{16,12},{20,16},{24,20},{28,24},{5,1},{9,5},{13... | collective-permute-start | bytes 73736 | tf_op jit(solution)/shard_map/ppermute | solution.py:19
  29.6 36.6 %copy-start.5 = (s32[4]{0:T(128)S(1)}, s32[4]{0:T(128)}, u32[]{:S(2)}) copy-start(s32[4]{0:T(128)} %param.15) | copy-start | bytes 52
  36.1 5.8 %collective-permute-start.2 = (f32[2,4,4,128]{3,2,1,0:T(4,128)S(1)}, f32[2,4,4,128]{3,2,1,0:T(4,128)S(1)}, u32[]{:S(2)}, u32[]{:S(2)}) collective-permute-start(f32[2,4,4,128]{3,2,1,0:T(4,128)S(1)} %get-tuple-element.7), channel_id=1, source_target_pairs={{0,4},{4,8},{8,12},{12,16},{16,20},{20,24},{24,28},{1,5},{5,9},{9,... | collective-permute-start | bytes 49160 | tf_op jit(solution)/shard_map/ppermute | solution.py:18
  40.4 5.6 %collective-permute-start.3 = (f32[2,4,4,128]{3,2,1,0:T(4,128)S(1)}, f32[2,4,4,128]{3,2,1,0:T(4,128)S(1)}, u32[]{:S(2)}, u32[]{:S(2)}) collective-permute-start(f32[2,4,4,128]{3,2,1,0:T(4,128)S(1)} %get-tuple-element.8), channel_id=1, source_target_pairs={{4,0},{8,4},{12,8},{16,12},{20,16},{24,20},{28,24},{5,1},{9,5},{13... | collective-permute-start | bytes 49160 | tf_op jit(solution)/shard_map/ppermute | solution.py:19
  46.9 32.9 %copy-start.2 = (f32[4,8,128]{2,1,0:T(8,128)S(1)}, f32[4,8,128]{2,1,0:T(8,128)}, u32[]{:S(2)}) copy-start(f32[4,8,128]{2,1,0:T(8,128)} %param.18) | copy-start | bytes 49156
  55.3 66.6 %copy-start.1 = (f32[7,7]{1,0:T(8,128)S(1)}, f32[7,7]{1,0:T(8,128)}, u32[]{:S(2)}) copy-start(f32[7,7]{1,0:T(8,128)} %constant.87.clone) | copy-start | bytes 592
  55.3 71.2 %copy-start = (f32[4,8,128]{2,1,0:T(8,128)S(1)}, f32[4,8,128]{2,1,0:T(8,128)}, u32[]{:S(2)}) copy-start(f32[4,8,128]{2,1,0:T(8,128)} %param.17) | copy-start | bytes 49156
  55.3 71.8 %copy-start.3 = (f32[4,8,128]{2,1,0:T(8,128)S(1)}, f32[4,8,128]{2,1,0:T(8,128)}, u32[]{:S(2)}) copy-start(f32[4,8,128]{2,1,0:T(8,128)} %param.16) | copy-start | bytes 49156
  61.5 4.8 %collective-permute-start.4 = (f32[1,4,4,128]{3,2,1,0:T(4,128)S(1)}, f32[1,4,4,128]{3,2,1,0:T(4,128)S(1)}, u32[]{:S(2)}, u32[]{:S(2)}) collective-permute-start(f32[1,4,4,128]{3,2,1,0:T(4,128)S(1)} %get-tuple-element.9), channel_id=1, source_target_pairs={{0,4},{4,8},{8,12},{12,16},{16,20},{20,24},{24,28},{1,5},{5,9},{9,... | collective-permute-start | bytes 24584 | tf_op jit(solution)/shard_map/ppermute | solution.py:18
  64.9 5.5 %collective-permute-start.5 = (f32[1,4,4,128]{3,2,1,0:T(4,128)S(1)}, f32[1,4,4,128]{3,2,1,0:T(4,128)S(1)}, u32[]{:S(2)}, u32[]{:S(2)}) collective-permute-start(f32[1,4,4,128]{3,2,1,0:T(4,128)S(1)} %get-tuple-element.10), channel_id=1, source_target_pairs={{4,0},{8,4},{12,8},{16,12},{20,16},{24,20},{28,24},{5,1},{9,5},{13... | collective-permute-start | bytes 24584 | tf_op jit(solution)/shard_map/ppermute | solution.py:19
where the time goes:
time: 128 us
  blocking collectives  58.7 us (46%)
  matrix products  30.5 us (24%)
  starting transfers between devices  15.2 us (12%)
  waiting for transfers between devices  10.9 us (9%)
  local copies, waits for them, and re-layouts  6.71 us (5%)
  other arithmetic  4.71 us (4%)
    psum x1, blocking collectives, body(): lax.psum(jnp.einsum('icbt,jcbt->cij', basis_stack, basis_stack, precision...  41.2 us
    dot_general x3, matrix products, multiply(): jnp.einsum('tij,kctj->kcti', tile_values, picked, precision=highest)  25.5 us
    all_gather x3, blocking collectives, apply_operator(): whole_part = lax.all_gather(stacked, 'rhs', axis=2, tiled=True)  17.5 us
    ppermute x3, starting transfers between devices, with_halo(): before = lax.ppermute(last, axis, up)  11.4 us
    ppermute x3, waiting for transfers between devices, with_halo(): after = lax.ppermute(first, axis, down)  10.7 us
    ppermute x3, starting transfers between devices, with_halo(): after = lax.ppermute(first, axis, down)  3.88 us
  transfers between devices with their start and end apart: 6, of which 4 were waited for; matrix products, arithmetic and copies ran while one was open for 2% of the time, Pallas kernels for 0%

commit v1 on v0

--- a/solution.py
+++ b/solution.py
@@ -130,9 +130,9 @@
     basis_stack, start_image = basis_from(
         apply_operator, direction_part, residual_part, [iterate_part]
     )
-    gram_matrix = lax.psum(
-        jnp.einsum("icbt,jcbt->cij", basis_stack, basis_stack, precision=highest), ("dom", "rhs")
-    )
+    gram_matrix = jnp.einsum("icbt,jcbt->cij", basis_stack, basis_stack, precision=highest)
+    for over in ("rhs", "dom"):
+        gram_matrix = lax.psum(gram_matrix, over)
     iterate_coef, residual_coef, direction_coef = coefficients(gram_matrix, SSTEP)
     new_iterate = iterate_part + combine(basis_stack, iterate_coef)
     recursive = combine(basis_stack, residual_coef)

time: 128 us -> 133 us (1.039)
  blocking collectives: 58.7 us -> 62.9 us
    psum x1 -> x2, blocking collectives: 41.2 us -> 45.4 us  [body(): gram_matrix = lax.psum(gram_matrix, over)]
where the time goes in v1:
time: 133 us; the launch traced here: 132 us
  blocking collectives  62.9 us (47%)
  matrix products  30.5 us (23%)
  starting transfers between devices  15.2 us (11%)
  waiting for transfers between devices  10.9 us (8%)
  local copies, waits for them, and re-layouts  6.71 us (5%)
  other arithmetic  4.7 us (4%)
    psum x2, blocking collectives, body(): gram_matrix = lax.psum(gram_matrix, over)  45.4 us
    dot_general x3, matrix products, multiply(): jnp.einsum('tij,kctj->kcti', tile_values, picked, precision=highest)  25.5 us
    all_gather x3, blocking collectives, apply_operator(): whole_part = lax.all_gather(stacked, 'rhs', axis=2, tiled=True)  17.5 us
    ppermute x3, starting transfers between devices, with_halo(): before = lax.ppermute(last, axis, up)  11.4 us
    ppermute x3, waiting for transfers between devices, with_halo(): after = lax.ppermute(first, axis, down)  10.7 us
    ppermute x3, starting transfers between devices, with_halo(): after = lax.ppermute(first, axis, down)  3.88 us
  transfers between devices with their start and end apart: 6, of which 4 were waited for; matrix products, arithmetic and copies ran while one was open for 2% of the time, Pallas kernels for 0%

profile of v1, /device:TPU:0, one launch (start us, length us, event | category | flops | bytes accessed | tf_op | source)
XLA Modules:
  0.0 131.9 jit_solution(12613601301889497057)
XLA Ops:
  0.6 0.8 reshape_squeeze.6
  1.4 0.8 reshape_squeeze.5
  2.2 0.8 pad_maximum_fusion.2
  2.9 6.8 %all_gather.9 = f32[3,4,32,128]{3,2,1,0:T(8,128)S(1)} all-gather(f32[3,4,8,128]{3,2,1,0:T(8,128)S(1)} %pad_maximum_fusion.2), channel_id=1, replica_groups=mesh['dom'=8,'rhs'=4] {'rhs'}, dimensions={2}, use_global_device_ids=true | all-gather | bytes 245760 | tf_op jit(solution)/shard_map/all_gather | solution.py:120
  9.8 0.1 copy.18
  9.9 0.6 gather_fusion
  10.5 0.1 fusion.31
  10.6 3.6 %collective-permute-start = (f32[3,4,4,128]{3,2,1,0:T(4,128)S(1)}, f32[3,4,4,128]{3,2,1,0:T(4,128)S(1)}, u32[]{:S(2)}, u32[]{:S(2)}) collective-permute-start(f32[3,4,4,128]{3,2,1,0:T(4,128)S(1)} %get-tuple-element.3), channel_id=1, source_target_pairs={{0,4},{4,8},{8,12},{12,16},{16,20},{20,24},{24,28},{1,5},{5,9},{9,... | collective-permute-start | bytes 73736 | tf_op jit(solution)/shard_map/ppermute | solution.py:18
  14.3 1.3 collective-permute-start.1
  15.6 0.7 compare_select_fusion.2
  16.2 0.7 compare_and_fusion.1
  16.9 0.7 constant_dynamic-update-slice_fusion.2
  17.6 2.3 %collective-permute-done.1 = f32[3,4,4,128]{3,2,1,0:T(4,128)S(1)} collective-permute-done((f32[3,4,4,128]{3,2,1,0:T(4,128)S(1)}, f32[3,4,4,128]{3,2,1,0:T(4,128)S(1)}, u32[]{:S(2)}, u32[]{:S(2)}) %collective-permute-start.1) | collective-permute-done | bytes 24608 | tf_op jit(solution)/shard_map/ppermute | solution.py:19
  20.1 0.8 gather_fusion.1
  20.9 8.7 %fusion.2 = f32[64,3,4,128]{3,2,1,0:T(4,128)S(1)} fusion(f32[64,128,128]{2,1,0:T(8,128)} %param.11, f32[64,3,4,128]{3,2,1,0:T(4,128)S(1)} %gather_fusion.1, pred[64]{0:T(512)(128)(4,1)S(1)} %compare_and_fusion.1), kind=kOutput, calls=%fused_computation.8 | convolution fusion | flops 151093248 | bytes 4980800 | tf_op jit(solution)/shard_map/tij,kctj->kcti/dot_general | solution.py:64
  29.6 0.3 convolution_bitcast_fusion.1
  29.9 5.4 %all_gather.10 = f32[2,4,32,128]{3,2,1,0:T(8,128)S(1)} all-gather(f32[2,4,8,128]{3,2,1,0:T(8,128)S(1)} %stack.26), channel_id=1, replica_groups=mesh['dom'=8,'rhs'=4] {'rhs'}, dimensions={2}, use_global_device_ids=true | all-gather | bytes 163840 | tf_op jit(solution)/shard_map/all_gather | solution.py:120
  35.3 0.1 copy.21
  35.4 0.6 gather_fusion.2
  36.0 0.1 fusion.32
  36.1 4.3 %collective-permute-start.2 = (f32[2,4,4,128]{3,2,1,0:T(4,128)S(1)}, f32[2,4,4,128]{3,2,1,0:T(4,128)S(1)}, u32[]{:S(2)}, u32[]{:S(2)}) collective-permute-start(f32[2,4,4,128]{3,2,1,0:T(4,128)S(1)} %get-tuple-element.7), channel_id=1, source_target_pairs={{0,4},{4,8},{8,12},{12,16},{16,20},{20,24},{24,28},{1,5},{5,9},{9,... | collective-permute-start | bytes 49160 | tf_op jit(solution)/shard_map/ppermute | solution.py:18
  40.4 1.3 collective-permute-start.3
  41.7 0.1 collective-permute-done.2
  41.8 4.2 %collective-permute-done.3 = f32[2,4,4,128]{3,2,1,0:T(4,128)S(1)} collective-permute-done((f32[2,4,4,128]{3,2,1,0:T(4,128)S(1)}, f32[2,4,4,128]{3,2,1,0:T(4,128)S(1)}, u32[]{:S(2)}, u32[]{:S(2)}) %collective-permute-start.3) | collective-permute-done | bytes 16416 | tf_op jit(solution)/shard_map/ppermute | solution.py:19
  46.1 0.7 gather_fusion.3
  46.9 8.4 %fusion = f32[64,2,4,128]{3,2,1,0:T(4,128)S(1)} fusion(f32[64,128,128]{2,1,0:T(8,128)} %param.11, f32[64,2,4,128]{3,2,1,0:T(4,128)S(1)} %gather_fusion.3, pred[64]{0:T(512)(128)(4,1)S(1)} %compare_and_fusion.1), kind=kOutput, calls=%fused_computation.6 | convolution fusion | flops 100728832 | bytes 4718656 | tf_op jit(solution)/shard_map/tij,kctj->kcti/dot_general | solution.py:64
  55.3 0.2 convolution_bitcast_fusion.2
  55.5 5.2 %all_gather.11 = f32[1,4,32,128]{3,2,1,0:T(8,128)S(1)} all-gather(f32[1,4,8,128]{3,2,1,0:T(8,128)S(1)} %get-tuple-element.5), channel_id=1, replica_groups=mesh['dom'=8,'rhs'=4] {'rhs'}, dimensions={2}, use_global_device_ids=true | all-gather | bytes 81920 | tf_op jit(solution)/shard_map/all_gather | solution.py:120
  60.8 0.6 gather_fusion.4
  61.4 0.1 bitcast_select_fusion
  61.5 3.4 %collective-permute-start.4 = (f32[1,4,4,128]{3,2,1,0:T(4,128)S(1)}, f32[1,4,4,128]{3,2,1,0:T(4,128)S(1)}, u32[]{:S(2)}, u32[]{:S(2)}) collective-permute-start(f32[1,4,4,128]{3,2,1,0:T(4,128)S(1)} %get-tuple-element.9), channel_id=1, source_target_pairs={{0,4},{4,8},{8,12},{12,16},{16,20},{20,24},{24,28},{1,5},{5,9},{9,... | collective-permute-start | bytes 24584 | tf_op jit(solution)/shard_map/ppermute | solution.py:18
  64.9 1.3 collective-permute-start.5
  66.3 4.2 %collective-permute-done.5 = f32[1,4,4,128]{3,2,1,0:T(4,128)S(1)} collective-permute-done((f32[1,4,4,128]{3,2,1,0:T(4,128)S(1)}, f32[1,4,4,128]{3,2,1,0:T(4,128)S(1)}, u32[]{:S(2)}, u32[]{:S(2)}) %collective-permute-start.5) | collective-permute-done | bytes 8224 | tf_op jit(solution)/shard_map/ppermute | solution.py:19
  70.5 0.7 gather_fusion.5
  71.2 8.4 %convolution_bitcast_fusion = f32[4,64,128]{2,0,1:T(4,128)S(1)} fusion(f32[64,128,128]{2,1,0:T(8,128)} %param.11, f32[64,4,128]{2,1,0:T(4,128)S(1)} %gather_fusion.5, pred[64]{0:T(512)(128)(4,1)S(1)} %compare_and_fusion.1), kind=kOutput, calls=%fused_computation.10 | convolution fusion | flops 50364416 | bytes 4456512 | tf_op jit(solution)/shard_map/tij,kctj->kcti/dot_general | solution.py:64
  79.5 0.2 fusion.4
  79.8 0.4 convolution_bitcast_fusion.3
  80.2 10.1 %psum.14 = f32[4,7,7]{2,1,0:T(8,128)S(1)} all-reduce(f32[4,7,7]{2,1,0:T(8,128)S(1)} %convolution_bitcast_fusion.3), channel_id=1, replica_groups=mesh['dom'=8,'rhs'=4] {'rhs'}, use_global_device_ids=true, to_apply=%region_0.1 | all-reduce | flops 196 | bytes 1568 | tf_op jit(solution)/shard_map/psum | solution.py:135
  90.3 35.3 %psum.15 = f32[4,7,7]{2,1,0:T(8,128)S(1)} all-reduce(f32[4,7,7]{2,1,0:T(8,128)S(1)} %psum.14), channel_id=1, replica_groups=mesh['dom'=8,'rhs'=4] {'dom'}, use_global_device_ids=true, to_apply=%region_1.2 | all-reduce | flops 196 | bytes 1568 | tf_op jit(solution)/shard_map/psum | solution.py:135
  125.6 0.2 fusion.53
  125.8 0.1 multiply_reduce_fusion.6
  125.9 0.2 fusion.54
  126.0 0.2 multiply_reduce_fusion.5
  126.4 0.2 fusion.55
  126.6 0.2 multiply_reduce_fusion.4
  126.8 0.1 multiply_add_fusion.3
  126.8 0.2 fusion.56
  127.0 0.2 multiply_reduce_fusion.3
  127.3 0.1 multiply_subtract_fusion.1
  127.3 0.2 fusion.57
  127.5 0.1 multiply_reduce_fusion.2
  127.6 0.1 multiply_add_fusion.2
  127.7 0.2 fusion.58
  127.9 0.2 multiply_reduce_fusion.1
  128.2 0.2 fusion.60
  128.4 0.1 multiply_reduce_fusion
  128.5 0.1 multiply_add_fusion
  128.6 0.9 fusion.15
  129.5 0.1 fusion.59
  129.7 0.3 fusion.19
  130.0 0.3 fusion.17
  130.3 0.3 fusion.21
  130.6 0.6 add.84
  131.3 0.7 fusion.35
  (48 shorter events, 0.6 us)
Async XLA Ops:
  0.6 29.0 %copy-start.4 = (s32[64]{0:T(128)S(1)}, s32[64]{0:T(128)}, u32[]{:S(2)}) copy-start(s32[64]{0:T(128)} %param.12) | copy-start | bytes 772
  10.6 7.0 %collective-permute-start = (f32[3,4,4,128]{3,2,1,0:T(4,128)S(1)}, f32[3,4,4,128]{3,2,1,0:T(4,128)S(1)}, u32[]{:S(2)}, u32[]{:S(2)}) collective-permute-start(f32[3,4,4,128]{3,2,1,0:T(4,128)S(1)} %get-tuple-element.3), channel_id=1, source_target_pairs={{0,4},{4,8},{8,12},{12,16},{16,20},{20,24},{24,28},{1,5},{5,9},{9,... | collective-permute-start | bytes 73736 | tf_op jit(solution)/shard_map/ppermute | solution.py:18
  14.3 5.7 %collective-permute-start.1 = (f32[3,4,4,128]{3,2,1,0:T(4,128)S(1)}, f32[3,4,4,128]{3,2,1,0:T(4,128)S(1)}, u32[]{:S(2)}, u32[]{:S(2)}) collective-permute-start(f32[3,4,4,128]{3,2,1,0:T(4,128)S(1)} %get-tuple-element.4), channel_id=1, source_target_pairs={{4,0},{8,4},{12,8},{16,12},{20,16},{24,20},{28,24},{5,1},{9,5},{13... | collective-permute-start | bytes 73736 | tf_op jit(solution)/shard_map/ppermute | solution.py:19
  29.6 36.6 %copy-start.5 = (s32[4]{0:T(128)S(1)}, s32[4]{0:T(128)}, u32[]{:S(2)}) copy-start(s32[4]{0:T(128)} %param.15) | copy-start | bytes 52
  36.1 5.8 %collective-permute-start.2 = (f32[2,4,4,128]{3,2,1,0:T(4,128)S(1)}, f32[2,4,4,128]{3,2,1,0:T(4,128)S(1)}, u32[]{:S(2)}, u32[]{:S(2)}) collective-permute-start(f32[2,4,4,128]{3,2,1,0:T(4,128)S(1)} %get-tuple-element.7), channel_id=1, source_target_pairs={{0,4},{4,8},{8,12},{12,16},{16,20},{20,24},{24,28},{1,5},{5,9},{9,... | collective-permute-start | bytes 49160 | tf_op jit(solution)/shard_map/ppermute | solution.py:18
  40.4 5.6 %collective-permute-start.3 = (f32[2,4,4,128]{3,2,1,0:T(4,128)S(1)}, f32[2,4,4,128]{3,2,1,0:T(4,128)S(1)}, u32[]{:S(2)}, u32[]{:S(2)}) collective-permute-start(f32[2,4,4,128]{3,2,1,0:T(4,128)S(1)} %get-tuple-element.8), channel_id=1, source_target_pairs={{4,0},{8,4},{12,8},{16,12},{20,16},{24,20},{28,24},{5,1},{9,5},{13... | collective-permute-start | bytes 49160 | tf_op jit(solution)/shard_map/ppermute | solution.py:19
  46.9 32.9 %copy-start.2 = (f32[4,8,128]{2,1,0:T(8,128)S(1)}, f32[4,8,128]{2,1,0:T(8,128)}, u32[]{:S(2)}) copy-start(f32[4,8,128]{2,1,0:T(8,128)} %param.18) | copy-start | bytes 49156
  55.3 70.8 %copy-start.1 = (f32[7,7]{1,0:T(8,128)S(1)}, f32[7,7]{1,0:T(8,128)}, u32[]{:S(2)}) copy-start(f32[7,7]{1,0:T(8,128)} %constant.87.clone) | copy-start | bytes 592
  55.3 75.3 %copy-start = (f32[4,8,128]{2,1,0:T(8,128)S(1)}, f32[4,8,128]{2,1,0:T(8,128)}, u32[]{:S(2)}) copy-start(f32[4,8,128]{2,1,0:T(8,128)} %param.17) | copy-start | bytes 49156
  55.3 75.9 %copy-start.3 = (f32[4,8,128]{2,1,0:T(8,128)S(1)}, f32[4,8,128]{2,1,0:T(8,128)}, u32[]{:S(2)}) copy-start(f32[4,8,128]{2,1,0:T(8,128)} %param.16) | copy-start | bytes 49156
  61.5 4.8 %collective-permute-start.4 = (f32[1,4,4,128]{3,2,1,0:T(4,128)S(1)}, f32[1,4,4,128]{3,2,1,0:T(4,128)S(1)}, u32[]{:S(2)}, u32[]{:S(2)}) collective-permute-start(f32[1,4,4,128]{3,2,1,0:T(4,128)S(1)} %get-tuple-element.9), channel_id=1, source_target_pairs={{0,4},{4,8},{8,12},{12,16},{16,20},{20,24},{24,28},{1,5},{5,9},{9,... | collective-permute-start | bytes 24584 | tf_op jit(solution)/shard_map/ppermute | solution.py:18
  64.9 5.5 %collective-permute-start.5 = (f32[1,4,4,128]{3,2,1,0:T(4,128)S(1)}, f32[1,4,4,128]{3,2,1,0:T(4,128)S(1)}, u32[]{:S(2)}, u32[]{:S(2)}) collective-permute-start(f32[1,4,4,128]{3,2,1,0:T(4,128)S(1)} %get-tuple-element.10), channel_id=1, source_target_pairs={{4,0},{8,4},{12,8},{16,12},{20,16},{24,20},{28,24},{5,1},{9,5},{13... | collective-permute-start | bytes 24584 | tf_op jit(solution)/shard_map/ppermute | solution.py:19
